TPU v7x, 32 devices: a whole 2x2x4 slice. The times are simulated.
32 devices in a mesh: cand: 4 (over x, core), seq: 8 (over z, y).
Axes of the slice: x: 2, y: 2, z: 4, core: 2. Of those that a mesh axis runs over, the one named last changes fastest.
Arguments:
- latent: bfloat16 [4, 384, 3072], P('cand', 'seq'), may hold values from -0.59765625 to 0.59765625
- timesteps: int32 [4], replicated, may hold values from 0 to 999
- positions: int32 [3, 384], replicated, may hold values from 0 to 63
- mod_weight: bfloat16 [3072, 9216], P('cand', 'seq'), may hold values from -0.109375 to 0.109375
- input_weight: bfloat16 [3072, 16, 384], P('cand', 'seq'), may hold values from -0.109375 to 0.109375
- output_weight: bfloat16 [16, 128, 3072], P('seq', None, 'cand'), may hold values from -0.75 to 0.75
- cotangent: bfloat16 [4, 384, 3072], P('cand', 'seq'), may hold values from -6 to 6
Outputs:
- block_out: bfloat16 [4, 384, 3072], P('cand', 'seq')
- latent_grad: float32 [4, 384, 3072], P('cand', 'seq')
All inputs are finite; a program needn't handle non-finite values.
Results may differ from a plain program's by a relative error of at most 0.033.
Values may be sent and summed in bfloat16 or wider, within the bound.
A program may use at most 128 MiB of HBM per device.

v0:
```python
import jax
import jax.numpy as jnp
import numpy as np
from jax import lax
from jax.sharding import PartitionSpec as P

HEAD = 128
epsilon = 1e-06


def time_embed(timesteps, feature_width):
    half_size = feature_width // 2
    freq_rate = jnp.exp(-jnp.log(10000.0) * jnp.arange(half_size, dtype=jnp.float32) / half_size)
    angles = timesteps.astype(jnp.float32)[:, None] * freq_rate[None, :]
    return jnp.concatenate([jnp.cos(angles), jnp.sin(angles)], axis=1)


def rope_tables(positions, head_size):
    first_size = head_size // 8
    other_size = (head_size - first_size) // 2
    pieces = []
    swapped = []
    sign_vec = []
    offset = 0
    for axis_id, width_part in enumerate((first_size, other_size, other_size)):
        half_size = width_part // 2
        freq_rate = jnp.exp(
            -jnp.log(256.0) * 2.0 * jnp.arange(half_size, dtype=jnp.float32) / width_part
        )
        angle_part = positions[axis_id].astype(jnp.float32)[:, None] * freq_rate[None, :]
        pieces.append(angle_part)
        pieces.append(angle_part)
        swapped += list(range(offset + half_size, offset + width_part)) + list(
            range(offset, offset + half_size)
        )
        sign_vec += [-1.0] * half_size + [1.0] * half_size
        offset += width_part
    angles = jnp.concatenate(pieces, axis=1)
    return (
        jnp.cos(angles),
        jnp.sin(angles),
        np.array(swapped, np.int32),
        np.array(sign_vec, np.float32),
    )


def rotate(values, tables):
    cos_tab, sin_tab, swapped, sign_vec = tables
    return values * cos_tab + values[..., swapped] * sign_vec * sin_tab


def unrotate(values, tables):
    cos_tab, sin_tab, swapped, sign_vec = tables
    return values * cos_tab - (values * sin_tab)[..., swapped] * sign_vec


def rms_norm(values):
    inverse = lax.rsqrt(jnp.mean(values * values, -1, keepdims=True) + epsilon)
    return (values * inverse, inverse)


def rms_back(d_normed, normed, inverse):
    return inverse * (d_normed - normed * jnp.mean(d_normed * normed, -1, keepdims=True))


def layer_norm(values):
    centred = values - jnp.mean(values, -1, keepdims=True)
    inverse_std = lax.rsqrt(jnp.mean(centred * centred, -1, keepdims=True) + epsilon)
    return (centred * inverse_std, inverse_std)


def layer_norm_back(d_normed, normed, inverse_std):
    return inverse_std * (
        d_normed
        - jnp.mean(d_normed, -1, keepdims=True)
        - normed * jnp.mean(d_normed * normed, -1, keepdims=True)
    )


def times_transposed(left, right):
    return lax.dot_general(
        left, right, (((1,), (1,)), ((), ())), preferred_element_type=jnp.float32
    )


def attend(projected, tables):
    length, groups, triple = projected.shape
    head_size = triple // 3
    grouped = jnp.transpose(projected.reshape(length, groups, 3, head_size), (2, 1, 0, 3))
    query_n, query_inv = rms_norm(grouped[0])
    key_n, key_inv = rms_norm(grouped[1])
    q_rot = rotate(query_n, tables).astype(jnp.bfloat16)
    k_rot = rotate(key_n, tables).astype(jnp.bfloat16)
    values = grouped[2].astype(jnp.bfloat16)
    score_scale = head_size ** (-0.5)
    scores = (
        jnp.einsum("gld,gmd->glm", q_rot, k_rot, preferred_element_type=jnp.float32) * score_scale
    )
    weights = jnp.exp(scores - head_size**0.5)
    probs = weights / jnp.sum(weights, -1, keepdims=True)
    probs_low = probs.astype(jnp.bfloat16)
    heads_out = jnp.einsum("glm,gmd->gld", probs_low, values, preferred_element_type=jnp.float32)
    attended = (
        jnp.transpose(heads_out, (1, 0, 2)).reshape(length, groups * head_size).astype(jnp.bfloat16)
    )
    saved = (q_rot, k_rot, values, probs, probs_low, query_n, query_inv, key_n, key_inv)
    return (attended, saved)


def attend_back(d_attended, saved, tables):
    q_rot, k_rot, values, probs, probs_low, query_n, query_inv, key_n, key_inv = saved
    groups, length, head_size = q_rot.shape
    score_scale = head_size ** (-0.5)
    d_heads = jnp.transpose(d_attended.reshape(length, groups, head_size), (1, 0, 2))
    d_values = jnp.einsum("glm,gld->gmd", probs_low, d_heads, preferred_element_type=jnp.float32)
    d_probs = jnp.einsum("gld,gmd->glm", d_heads, values, preferred_element_type=jnp.float32)
    d_scores = (probs * (d_probs - jnp.sum(probs * d_probs, -1, keepdims=True))).astype(
        jnp.bfloat16
    )
    d_qrot = (
        jnp.einsum("glm,gmd->gld", d_scores, k_rot, preferred_element_type=jnp.float32)
        * score_scale
    )
    d_krot = (
        jnp.einsum("glm,gld->gmd", d_scores, q_rot, preferred_element_type=jnp.float32)
        * score_scale
    )
    d_query = rms_back(unrotate(d_qrot, tables), query_n, query_inv)
    d_key = rms_back(unrotate(d_krot, tables), key_n, key_inv)
    stacked = jnp.stack([d_query, d_key, d_values], 0)
    return (
        jnp.transpose(stacked, (2, 1, 0, 3))
        .reshape(length, groups * 3 * head_size)
        .astype(jnp.bfloat16)
    )


def on_device(latent, timesteps, positions, mod_weight, input_weight, output_weight, cotangent):
    width = latent.shape[2]
    rows_local = latent.shape[1]
    groups = input_weight.shape[1]
    group_cols = groups * input_weight.shape[2]
    time_act = jax.nn.silu(time_embed(timesteps, width)).astype(jnp.bfloat16)
    slab_rows = mod_weight.shape[0]
    act_rows = lax.dynamic_slice_in_dim(time_act, lax.axis_index("cand") * slab_rows, slab_rows, 1)
    mod_mine = lax.psum_scatter(
        jnp.dot(act_rows, mod_weight, preferred_element_type=jnp.float32).astype(jnp.bfloat16),
        "cand",
        scatter_dimension=0,
        tiled=True,
    ).astype(jnp.float32)
    modulation = lax.all_gather(mod_mine, "seq", axis=1, tiled=True)[0]
    shift_vec = modulation[:width]
    scale_vec = modulation[width : 2 * width]
    gate_vec = modulation[2 * width :]
    latent_rows = latent[0].astype(jnp.float32)
    normed, inverse_std = layer_norm(latent_rows)
    modulated = (normed * (1.0 + scale_vec) + shift_vec).astype(jnp.bfloat16)
    gathered = lax.all_gather(modulated, "seq", axis=0, tiled=True)
    length = gathered.shape[0]
    tables = rope_tables(positions, HEAD)
    piece = lax.all_gather(input_weight, "cand", axis=0, tiled=True)
    projected = jnp.dot(
        gathered, piece.reshape(piece.shape[0], group_cols), preferred_element_type=jnp.float32
    )
    attended, saved = attend(projected.reshape(length, groups, 3 * HEAD), tables)
    w_heads = lax.all_gather(output_weight, "seq", axis=0, tiled=True)
    w_all = lax.all_gather(w_heads, "cand", axis=2, tiled=True)
    w_all = w_all.reshape(w_all.shape[0] * w_all.shape[1], width)
    token_heads = lax.all_to_all(attended, "seq", split_axis=0, concat_axis=1, tiled=True)
    mixed = jnp.dot(token_heads, w_all, preferred_element_type=jnp.float32)
    block_out = (latent_rows + gate_vec * mixed).astype(jnp.bfloat16)
    d_mixed = (cotangent[0].astype(jnp.float32) * gate_vec).astype(jnp.bfloat16)
    d_tokens = times_transposed(d_mixed, w_all).astype(jnp.bfloat16)
    d_attended = lax.all_to_all(d_tokens, "seq", split_axis=1, concat_axis=0, tiled=True)
    d_projected = attend_back(d_attended, saved, tables)
    w_back = lax.all_gather(input_weight, "cand", axis=0, tiled=True).reshape(width, group_cols)
    d_modulated = lax.psum_scatter(
        times_transposed(
            lax.slice_in_dim(d_projected, 0, rows_local * lax.axis_size("seq"), axis=0), w_back
        ).astype(jnp.bfloat16),
        "seq",
        scatter_dimension=0,
        tiled=True,
    ).astype(jnp.float32)
    latent_grad = cotangent[0].astype(jnp.float32) + layer_norm_back(
        d_modulated * (1.0 + scale_vec), normed, inverse_std
    )
    return (block_out[None], latent_grad[None])


def solution(mesh):
    placed = (
        P("cand", "seq", None),
        P(),
        P(),
        P("cand", "seq"),
        P("cand", "seq", None),
        P("seq", None, "cand"),
        P("cand", "seq", None),
    )
    return jax.shard_map(
        on_device,
        mesh=mesh,
        in_specs=placed,
        out_specs=(P("cand", "seq", None), P("cand", "seq", None)),
        check_vma=False,
    )
```

profile of v0, /device:TPU:0, one launch (start us, length us, event | category | flops | bytes accessed | tf_op | source)
XLA Modules:
  0.0 380.3 jit_solution(16041550091423698796)
XLA Ops:
  7.2 0.7 all-gather.9.cloned.1.call-update
  8.0 0.7 all-gather.7.cloned.1.call-update
  8.8 0.6 dynamic-slice
  9.7 0.3 convolution_convert_fusion.2
  10.0 8.7 %all-reduce = bf16[4,1152]{1,0:T(4,128)(2,1)S(1)} all-reduce(bf16[4,1152]{1,0:T(4,128)(2,1)S(1)} %convolution_convert_fusion.2), channel_id=2, replica_groups=mesh['cand'=4,'seq'=8] {'cand'}, use_global_device_ids=true, to_apply=%region_0.1.clone | all-reduce | flops 4608 | bytes 18432
  18.7 0.7 dynamic-slice_convert_fusion
  19.4 31.6 %all_gather.16 = f32[1,9216]{1,0:T(1,128)S(1)} all-gather(f32[1,1152]{1,0:T(1,128)S(1)} %dynamic-slice_convert_fusion), channel_id=1, replica_groups=mesh['cand'=4,'seq'=8] {'seq'}, dimensions={1}, use_global_device_ids=true | all-gather | bytes 41472 | tf_op jit(solution)/shard_map/all_gather | solution.py:152
  51.4 0.9 fusion.19
  52.4 20.8 %all-gather.9.cloned.1.call-done = bf16[16,128,768]{2,1,0:T(8,128)(2,1)} async-done(((bf16[2,128,768]{2,1,0:T(8,128)(2,1)}), bf16[16,128,768]{2,1,0:T(8,128)(2,1)}) %all-gather.9.cloned.1.call-update) | async-done | bytes 3145744 | tf_op jit(solution)/shard_map/all_gather | solution.py:167
  73.2 0.6 copy-done.25
  74.4 0.6 pad_clamp_fusion
  74.9 0.7 fusion.61
  75.6 0.8 broadcast_multiply_fusion.2
  76.4 34.5 %all-gather.7.cloned.1.call-done = bf16[3072,2,384]{2,1,0:T(2,128)(2,1)} async-done(((bf16[768,2,384]{2,1,0:T(2,128)(2,1)}), bf16[3072,2,384]{2,1,0:T(2,128)(2,1)}) %all-gather.7.cloned.1.call-update) | async-done | bytes 4718608 | tf_op jit(solution)/shard_map/all_gather | solution.py:162
  110.9 5.2 %copy.89 = bf16[384,8,2,384]{3,1,2,0:T(8,128)(2,1)} copy(bf16[384,8,2,384]{3,2,1,0:T(2,128)(2,1)} %bitcast.149) | data formatting | bytes 9437184
  116.1 6.7 %copy.50 = bf16[3072,768]{0,1:T(8,128)(2,1)} copy(bf16[3072,768]{1,0:T(8,128)(2,1)} %bitcast.145) | data formatting | bytes 9437184 | tf_op jit(solution)/shard_map/reshape | solution.py:164
  122.8 42.7 %all-gather.5.cloned.1.call-done = bf16[384,3072]{1,0:T(8,128)(2,1)} async-done(((bf16[48,3072]{1,0:T(8,128)(2,1)}), bf16[384,3072]{1,0:T(8,128)(2,1)}) %all-gather.5.cloned.1.call-update) | async-done | bytes 2359312 | tf_op jit(solution)/shard_map/all_gather | solution.py:159
  165.5 5.3 %fusion.5 = f32[3,2,384,128]{2,3,0,1:T(8,128)S(1)} fusion(bf16[2,3,128,3072]{3,2,1,0:T(8,128)(2,1)} %bitcast.150, bf16[384,3072]{1,0:T(8,128)(2,1)} %all-gather.5.cloned.1.call-done), kind=kOutput, calls=%fused_computation.13 | convolution fusion | flops 1811939328 | bytes 8257536 | tf_op jit(solution)/shard_map/dot_general | solution.py:163
  170.8 1.0 copy-done.6
  171.9 75.6 %all-gather.11.cloned.1.call-done = bf16[16,128,3072]{2,1,0:T(8,128)(2,1)} async-done(((bf16[16,128,768]{2,1,0:T(8,128)(2,1)}), bf16[16,128,3072]{2,1,0:T(8,128)(2,1)}) %all-gather.11.cloned.1.call-update) | async-done | bytes 12582928 | tf_op jit(solution)/shard_map/all_gather | solution.py:168
  247.6 8.5 %convolution_convert_fusion.1 = bf16[48,2048]{1,0:T(8,128)(2,1)S(1)} fusion(bf16[2048,3072]{1,0:T(8,128)(2,1)} %bitcast.143, bf16[1,48,3072]{2,1,0:T(8,128)(2,1)S(1)} %copy-done.10, f32[3072]{0:T(1024)S(1)} %bitcast.159), kind=kOutput, calls=%fused_computation.11 | convolution fusion | flops 604520448 | bytes 13086720 | tf_op jit(solution)/shard_map/dot_general | solution.py:81
  256.0 0.7 copy.119
  256.7 5.5 %all-to-all-start.1 = ((bf16[48,8,256]{2,0,1:T(8,128)(2,1)}), bf16[48,8,256]{2,0,1:T(8,128)(2,1)S(1)}, u32[]{:S(2)}, u32[]{:S(2)}) async-start(bf16[48,8,256]{2,0,1:T(8,128)(2,1)} %bitcast.142), calls=%async_computation.1 | async-start | bytes 393216 | tf_op jit(solution)/shard_map/all_to_all | solution.py:175
  262.5 1.2 fusion.35
  263.7 1.1 copy.52
  264.8 1.0 copy.54
  265.8 2.2 gather_fusion
  268.0 2.9 gather_fusion.1
  270.9 1.9 fusion.31
  272.9 2.5 fusion.45
  275.3 2.1 multiply_reduce_fusion
  277.5 1.1 fusion.11
  278.9 0.8 copy-done.14
  280.0 0.6 copy-done.13
  280.7 1.1 broadcast_multiply_fusion
  281.8 1.0 copy.69
  282.8 2.9 gather_fusion.3
  285.7 2.0 copy.66
  287.8 2.9 gather_fusion.2
  290.6 2.0 multiply_reduce_fusion.2
  292.7 2.0 fusion.41
  294.9 3.5 convolution_convert_fusion
  298.4 1.4 fusion.10
  300.2 18.7 %all_to_all.32 = bf16[8,48,256]{2,1,0:T(8,128)(2,1)S(1)} all-to-all(bf16[8,48,256]{2,1,0:T(8,128)(2,1)S(1)} %convert_element_type.131), channel_id=1, replica_groups=mesh['cand'=4,'seq'=8] {'seq'}, dimensions={0} | all-to-all | bytes 393216 | tf_op jit(solution)/shard_map/all_to_all | solution.py:170
  319.0 7.9 %fusion.2 = bf16[1,48,3072]{2,1,0:T(8,128)(2,1)} fusion(bf16[48,2048]{1,0:T(8,128)(2,1)S(1)} %bitcast.151, bf16[2048,3072]{1,0:T(8,128)(2,1)} %bitcast.144, bf16[1,48,3072]{2,1,0:T(8,128)(2,1)S(1)} %copy-done.2, f32[3072]{0:T(1024)S(1)} %bitcast.160), kind=kOutput, calls=%fused_computation.8 | convolution fusion | flops 604569600 | bytes 13381632 | tf_op jit(solution)/shard_map/dot_general | solution.py:171
  326.9 43.6 %reduce-scatter.2.cloned.1.call-done = bf16[48,3072]{1,0:T(8,128)(2,1)} async-done(((bf16[384,3072]{1,0:T(8,128)(2,1)}), bf16[48,3072]{1,0:T(8,128)(2,1)}) %reduce-scatter.2.cloned.1.call-update) | async-done | bytes 294928 | tf_op jit(solution)/shard_map/reduce_scatter | solution.py:178
  370.5 1.2 fusion.27
  371.8 2.0 fusion.24
  (96 shorter events, 3.1 us)
Async XLA Ops:
  7.2 2.5 copy-start
  7.2 1.6 copy-start.28
  7.2 1.6 copy-start.27
  7.2 66.0 %all-gather.9.cloned.1.call-start = ((), (), s32[]{:S(2)}) async-start(), calls=%async_computation.5 | async-start | bytes 3538944 | tf_op jit(solution)/shard_map/all_gather | solution.py:167
  7.9 103.0 %all-gather.7.cloned.1.call-start = ((), (), s32[]{:S(2)}) async-start(), calls=%async_computation.4 | async-start | bytes 5898240 | tf_op jit(solution)/shard_map/all_gather | solution.py:162
  8.7 42.3 %copy-start.1 = (bf16[1,48,3072]{2,1,0:T(8,128)(2,1)S(1)}, bf16[1,48,3072]{2,1,0:T(8,128)(2,1)}, u32[]{:S(2)}) copy-start(bf16[1,48,3072]{2,1,0:T(8,128)(2,1)} %param.13) | copy-start | bytes 884740
  8.7 156.8 %all-gather.5.cloned.1.call-start = ((), (), s32[]{:S(2)}) async-start(), calls=%async_computation.3 | async-start | bytes 2654208 | tf_op jit(solution)/shard_map/all_gather | solution.py:159
  51.1 22.1 %copy-start.20 = (f32[48]{0:T(128)}, f32[48]{0:T(128)S(1)}, u32[]{:S(2)}) copy-start(f32[48]{0:T(128)S(1)} %broadcast_multiply_fusion.11) | copy-start | bytes 580
  51.4 21.8 %copy-start.23 = (f32[48]{0:T(128)}, f32[48]{0:T(128)S(1)}, u32[]{:S(2)}) copy-start(f32[48]{0:T(128)S(1)} %add_rsqrt_fusion.2) | copy-start | bytes 580
  51.4 196.1 %copy-start.16 = (f32[1,3072]{1,0:T(1,128)}, f32[1,3072]{1,0:T(1,128)S(1)}, u32[]{:S(2)}) copy-start(f32[1,3072]{1,0:T(1,128)S(1)} %get-tuple-element.21) | copy-start | bytes 36868
  52.4 195.2 %all-gather.11.cloned.1.call-start = ((), (), s32[]{:S(2)}) async-start(), calls=%async_computation.6 | async-start | bytes 15728640 | tf_op jit(solution)/shard_map/all_gather | solution.py:168
  73.2 0.7 copy-start.25
  73.2 1.2 copy-start.26
  165.5 82.1 %copy-start.10 = (bf16[1,48,3072]{2,1,0:T(8,128)(2,1)S(1)}, bf16[1,48,3072]{2,1,0:T(8,128)(2,1)}, u32[]{:S(2)}) copy-start(bf16[1,48,3072]{2,1,0:T(8,128)(2,1)} %param.19) | copy-start | bytes 884740
  170.8 1.1 copy-start.6
  171.9 90.5 %copy-start.18 = (f32[2,384]{1,0:T(2,128)}, f32[2,384]{1,0:T(2,128)S(1)}, u32[]{:S(2)}) copy-start(f32[2,384]{1,0:T(2,128)S(1)} %get-tuple-element.32) | copy-start | bytes 9220
  256.7 16.1 %all-to-all-start.1 = ((bf16[48,8,256]{2,0,1:T(8,128)(2,1)}), bf16[48,8,256]{2,0,1:T(8,128)(2,1)S(1)}, u32[]{:S(2)}, u32[]{:S(2)}) async-start(bf16[48,8,256]{2,0,1:T(8,128)(2,1)} %bitcast.142), calls=%async_computation.1 | async-start | bytes 393216 | tf_op jit(solution)/shard_map/all_to_all | solution.py:175
  262.2 108.2 %reduce-scatter.2.cloned.1.call-start = ((), (), s32[]{:S(2)}) async-start(), calls=%async_computation.7 | async-start | bytes 2654208 | tf_op jit(solution)/shard_map/reduce_scatter | solution.py:178
  263.7 11.7 %copy-start.3 = (f32[2,384,128]{1,2,0:T(8,128)}, f32[2,384,128]{1,2,0:T(8,128)S(1)}, u32[]{:S(2)}) copy-start(f32[2,384,128]{1,2,0:T(8,128)S(1)} %get-tuple-element.11) | copy-start | bytes 1179652
  263.7 11.7 %copy-start.4 = (f32[2,384,128]{1,2,0:T(8,128)}, f32[2,384,128]{1,2,0:T(8,128)S(1)}, u32[]{:S(2)}) copy-start(f32[2,384,128]{1,2,0:T(8,128)S(1)} %get-tuple-element.12) | copy-start | bytes 1179652
  272.8 2.5 copy-start.8
  275.3 2.1 copy-start.9
  277.5 1.3 copy-start.7
  278.7 0.9 copy-start.14
  279.7 0.9 copy-start.13
  279.7 1.0 copy-start.15
  279.9 1.9 copy-start.5
  281.8 13.1 %slice-start = ((s8[4718592]{0:T(1024)(128)(4,1)}), s8[524288]{0:T(1024)(128)(4,1)S(1)}, s32[]{:S(2)}) async-start(s8[4718592]{0:T(1024)(128)(4,1)} %bitcast.146), calls=%async_computation.8 | async-start | bytes 1048576
  282.8 7.8 %copy-start.22 = (f32[128]{0:T(128)S(1)}, f32[128]{0:T(128)}, u32[]{:S(2)}) copy-start(f32[128]{0:T(128)} %constant.63.clone) | copy-start | bytes 1540
  287.8 4.9 %copy-start.19 = (f32[2,384]{1,0:T(2,128)S(1)}, f32[2,384]{1,0:T(2,128)}, u32[]{:S(2)}) copy-start(f32[2,384]{1,0:T(2,128)} %copy-done.18) | copy-start | bytes 9220
  290.6 4.2 %slice-start.1 = ((s8[4718592]{0:T(1024)(128)(4,1)}), s8[4194304]{0:T(1024)(128)(4,1)S(1)}, s32[]{:S(2)}) async-start(s8[4718592]{0:T(1024)(128)(4,1)} %bitcast.146), calls=%async_computation.9 | async-start | bytes 8388608
  292.7 2.0 copy-start.12
  299.8 19.1 %copy-start.2 = (bf16[1,48,3072]{2,1,0:T(8,128)(2,1)S(1)}, bf16[1,48,3072]{2,1,0:T(8,128)(2,1)}, u32[]{:S(2)}) copy-start(bf16[1,48,3072]{2,1,0:T(8,128)(2,1)} %param.13) | copy-start | bytes 884740
  299.8 19.1 %copy-start.17 = (f32[1,3072]{1,0:T(1,128)S(1)}, f32[1,3072]{1,0:T(1,128)}, u32[]{:S(2)}) copy-start(f32[1,3072]{1,0:T(1,128)} %copy-done.16) | copy-start | bytes 36868
  318.9 51.6 %copy-start.21 = (f32[48]{0:T(128)S(1)}, f32[48]{0:T(128)}, u32[]{:S(2)}) copy-start(f32[48]{0:T(128)} %copy-done.20) | copy-start | bytes 580
  318.9 51.6 %copy-start.24 = (f32[48]{0:T(128)S(1)}, f32[48]{0:T(128)}, u32[]{:S(2)}) copy-start(f32[48]{0:T(128)} %copy-done.23) | copy-start | bytes 580
  318.9 52.8 %copy-start.11 = (bf16[1,48,3072]{2,1,0:T(8,128)(2,1)S(1)}, bf16[1,48,3072]{2,1,0:T(8,128)(2,1)}, u32[]{:S(2)}) copy-start(bf16[1,48,3072]{2,1,0:T(8,128)(2,1)} %param.19) | copy-start | bytes 884740
Sparse Core Ops, SparseCore 0:
  10.2 62.9 all-gather.8
  74.7 36.1 all-gather.6
  113.7 51.8 all-gather.4
  166.9 80.6 all-gather.10
  298.5 71.9 reduce-scatter.1
where the time goes:
time: 381 us; the launch traced here: 380 us
  waiting for transfers between devices  219 us (57%)
  blocking collectives  59 us (15%)
  local copies, waits for them, and re-layouts  34.1 us (9%)
  matrix products  33.8 us (9%)
  other arithmetic  14.5 us (4%)
  between operations  14.3 us (4%)
  starting transfers between devices  5.89 us (2%)
    all_gather x1, waiting for transfers between devices, on_device(): w_all = lax.all_gather(w_heads, 'cand', axis=2, tiled=True)  75.6 us
    reduce_scatter x1, waiting for transfers between devices, on_device(): lax.psum_scatter(times_transposed(lax.slice_in_dim(d_projected, 0, rows_l...  43.6 us
    all_gather x1, waiting for transfers between devices, on_device(): gathered = lax.all_gather(modulated, 'seq', axis=0, tiled=True)  42.7 us
    all_gather x1, waiting for transfers between devices, on_device(): piece = lax.all_gather(input_weight, 'cand', axis=0, tiled=True)  34.5 us
    all_gather x1, blocking collectives, on_device(): modulation = lax.all_gather(mod_mine, 'seq', axis=1, tiled=True)[0]  31.6 us
    all_gather x1, waiting for transfers between devices, on_device(): w_heads = lax.all_gather(output_weight, 'seq', axis=0, tiled=True)  20.8 us
    all_to_all x1, blocking collectives, on_device(): lax.all_to_all(attended, 'seq', split_axis=0, concat_axis=1, tiled=True)  18.7 us
    dot_general x2, matrix products, times_transposed(): lax.dot_general(left, right, (((1,), (1,)), ((), ())), preferred_element_...  11.9 us
  transfers between devices with their start and end apart: 6, of which 5 were waited for; matrix products, arithmetic and copies ran while one was open for 11% of the time, Pallas kernels for 0%

commit v1 on v0

--- a/solution.py
+++ b/solution.py
@@ -159,7 +159,12 @@
     gathered = lax.all_gather(modulated, "seq", axis=0, tiled=True)
     length = gathered.shape[0]
     tables = rope_tables(positions, HEAD)
-    piece = lax.all_gather(input_weight, "cand", axis=0, tiled=True)
+    ring = [input_weight]
+    for hop in range(3):
+        ring.append(lax.ppermute(ring[-1], "cand", [(dev, (dev + 1) % 4) for dev in range(4)]))
+    piece = jnp.roll(
+        jnp.concatenate(ring[::-1], axis=0), (lax.axis_index("cand") + 1) * ring[0].shape[0], axis=0
+    )
     projected = jnp.dot(
         gathered, piece.reshape(piece.shape[0], group_cols), preferred_element_type=jnp.float32
     )

time: 381 us -> 360 us (0.945)
  waiting for transfers between devices: 219 us -> 194 us
  local copies, waits for them, and re-layouts: 34.1 us -> 39.1 us
    ppermute x0 -> x3, waiting for transfers between devices: none -> 45.2 us  [on_device(): lax.ppermute(ring[-1], 'cand', [(dev, (dev + 1) % 4) for dev in range(4)])]
    all_gather x1, waiting for transfers between devices: 42.7 us -> 0.01 us  [on_device(): gathered = lax.all_gather(modulated, 'seq', axis=0, tiled=True)]
    all_gather x1, waiting for transfers between devices: 34.5 us -> 15.1 us  [on_device(): lax.all_gather(input_weight, 'cand', axis=0, tiled=True)]
    all_gather x1, waiting for transfers between devices: 75.6 us -> 68.4 us  [on_device(): w_all = lax.all_gather(w_heads, 'cand', axis=2, tiled=True)]
    reshape x1 -> x0, local copies, waits for them, and re-layouts: 6.68 us -> none  [on_device(): piece.reshape(piece.shape[0], group_cols)]
    unnamed x64 -> x50, local copies, waits for them, and re-layouts: 9.31 us -> 15.4 us
    dynamic_slice x0 -> x1, local copies, waits for them, and re-layouts: none -> 4.98 us  [on_device(): jnp.roll(jnp.concatenate(ring[::-1], axis=0), (lax.axis_index('cand') + 1...]
  transfers between devices with their start and end apart: 6 -> 9, of which waited for: 5 -> 7; matrix products, arithmetic and copies ran while one was open for 11% -> 16% of each run, Pallas kernels for 0% -> 0%
where the time goes in v1:
time: 360 us; the launch traced here: 359 us
  waiting for transfers between devices  194 us (54%)
  blocking collectives  58.8 us (16%)
  local copies, waits for them, and re-layouts  39.1 us (11%)
  matrix products  35.7 us (10%)
  between operations  14.3 us (4%)
  other arithmetic  11 us (3%)
  starting transfers between devices  5.95 us (2%)
    all_gather x1, waiting for transfers between devices, on_device(): w_all = lax.all_gather(w_heads, 'cand', axis=2, tiled=True)  68.4 us
    ppermute x3, waiting for transfers between devices, on_device(): lax.ppermute(ring[-1], 'cand', [(dev, (dev + 1) % 4) for dev in range(4)])  45.2 us
    reduce_scatter x1, waiting for transfers between devices, on_device(): lax.psum_scatter(times_transposed(lax.slice_in_dim(d_projected, 0, rows_l...  44.1 us
    all_gather x1, blocking collectives, on_device(): modulation = lax.all_gather(mod_mine, 'seq', axis=1, tiled=True)[0]  31.5 us
    all_gather x1, waiting for transfers between devices, on_device(): w_heads = lax.all_gather(output_weight, 'seq', axis=0, tiled=True)  20.4 us
    all_to_all x1, blocking collectives, on_device(): lax.all_to_all(attended, 'seq', split_axis=0, concat_axis=1, tiled=True)  18.6 us
    unnamed x50, local copies, waits for them, and re-layouts  15.4 us
    all_gather x1, waiting for transfers between devices, on_device(): lax.all_gather(input_weight, 'cand', axis=0, tiled=True)  15.1 us
  transfers between devices with their start and end apart: 9, of which 7 were waited for; matrix products, arithmetic and copies ran while one was open for 16% of the time, Pallas kernels for 0%

profile of v1, /device:TPU:0, one launch (start us, length us, event | category | flops | bytes accessed | tf_op | source)
XLA Modules:
  0.0 358.8 jit_solution(6715885833117669812)
XLA Ops:
  7.2 0.7 all-gather.7.cloned.1.call-update
  8.0 0.7 convert_element_type.114
  8.6 1.2 dynamic-slice
  10.5 8.7 %all-reduce = bf16[4,1152]{1,0:T(4,128)(2,1)S(1)} all-reduce(bf16[4,1152]{1,0:T(4,128)(2,1)S(1)} %convolution_convert_fusion.2), channel_id=2, replica_groups=mesh['cand'=4,'seq'=8] {'cand'}, use_global_device_ids=true, to_apply=%region_0.1.clone | all-reduce | flops 4608 | bytes 18432
  19.2 0.7 dynamic-slice_convert_fusion
  19.9 31.5 %all_gather.15 = f32[1,9216]{1,0:T(1,128)S(1)} all-gather(f32[1,1152]{1,0:T(1,128)S(1)} %dynamic-slice_convert_fusion), channel_id=1, replica_groups=mesh['cand'=4,'seq'=8] {'seq'}, dimensions={1}, use_global_device_ids=true | all-gather | bytes 41472 | tf_op jit(solution)/shard_map/all_gather | solution.py:152
  51.8 0.9 fusion.19
  52.8 20.4 %all-gather.7.cloned.1.call-done = bf16[16,128,768]{2,1,0:T(8,128)(2,1)} async-done(((bf16[2,128,768]{2,1,0:T(8,128)(2,1)}), bf16[16,128,768]{2,1,0:T(8,128)(2,1)}) %all-gather.7.cloned.1.call-update) | async-done | bytes 3145744 | tf_op jit(solution)/shard_map/all_gather | solution.py:172
  73.3 2.0 copy.51
  75.3 15.6 %collective-permute-done = bf16[768,2,384]{0,2,1:T(8,128)(2,1)S(1)} collective-permute-done((bf16[768,2,384]{0,2,1:T(8,128)(2,1)S(1)}, bf16[768,2,384]{0,2,1:T(8,128)(2,1)S(1)}, u32[]{:S(2)}, u32[]{:S(2)}) %collective-permute-start) | collective-permute-done | bytes 1179680 | tf_op jit(solution)/shard_map/ppermute | solution.py:164
  90.9 15.7 %collective-permute-done.1 = bf16[768,2,384]{0,2,1:T(8,128)(2,1)} collective-permute-done((bf16[768,2,384]{0,2,1:T(8,128)(2,1)S(1)}, bf16[768,2,384]{0,2,1:T(8,128)(2,1)}, u32[]{:S(2)}, u32[]{:S(2)}) %collective-permute-start.1) | collective-permute-done | bytes 1179680 | tf_op jit(solution)/shard_map/ppermute | solution.py:164
  107.2 0.7 fusion.61
  107.9 0.7 broadcast_multiply_fusion.2
  108.7 13.9 %collective-permute-done.2 = bf16[768,2,384]{0,2,1:T(8,128)(2,1)} collective-permute-done((bf16[768,2,384]{0,2,1:T(8,128)(2,1)}, bf16[768,2,384]{0,2,1:T(8,128)(2,1)}, u32[]{:S(2)}, u32[]{:S(2)}) %collective-permute-start.2) | collective-permute-done | bytes 1179680 | tf_op jit(solution)/shard_map/ppermute | solution.py:164
  122.6 1.4 constant_dynamic-update-slice_fusion.7
  124.0 1.4 constant_dynamic-update-slice_fusion.6
  125.8 1.4 constant_dynamic-update-slice_fusion.3
  127.2 1.4 constant_dynamic-update-slice_fusion.2
  129.0 5.0 %constant_dynamic-slice_fusion = bf16[3072,2,384]{0,2,1:T(8,128)(2,1)} fusion(bf16[6144,2,384]{0,2,1:T(8,128)(2,1)S(1)} %constant_dynamic-update-slice_fusion, s32[]{:T(128)S(6)} %select_n.30), kind=kLoop, calls=%fused_computation.117 | loop fusion | bytes 9437188 | tf_op jit(solution)/shard_map/jit(_roll_dynamic)/dynamic_slice | solution.py:165
  134.0 6.1 %fusion.5 = f32[3,2,384,128]{2,3,0,1:T(8,128)S(1)} fusion(bf16[2,3,128,3072]{3,2,1,0:T(8,128)(2,1)} %bitcast.149, bf16[384,3072]{1,0:T(8,128)(2,1)} %all-gather.5.cloned.1.call-done), kind=kOutput, calls=%fused_computation.13 | convolution fusion | flops 1811939328 | bytes 8257536 | tf_op jit(solution)/shard_map/dot_general | solution.py:168
  140.2 68.4 %all-gather.9.cloned.1.call-done = bf16[16,128,3072]{2,1,0:T(8,128)(2,1)} async-done(((bf16[16,128,768]{2,1,0:T(8,128)(2,1)}), bf16[16,128,3072]{2,1,0:T(8,128)(2,1)}) %all-gather.9.cloned.1.call-update) | async-done | bytes 12582928 | tf_op jit(solution)/shard_map/all_gather | solution.py:173
  208.6 8.5 %convolution_convert_fusion.1 = bf16[48,2048]{1,0:T(8,128)(2,1)S(1)} fusion(bf16[2048,3072]{1,0:T(8,128)(2,1)} %bitcast.145, bf16[1,48,3072]{2,1,0:T(8,128)(2,1)S(1)} %copy-done.10, f32[3072]{0:T(1024)S(1)} %bitcast.157), kind=kOutput, calls=%fused_computation.11 | convolution fusion | flops 604520448 | bytes 13086720 | tf_op jit(solution)/shard_map/dot_general | solution.py:81
  217.1 0.7 copy.122
  217.8 5.5 %all-to-all-start.1 = ((bf16[48,8,256]{2,0,1:T(8,128)(2,1)}), bf16[48,8,256]{2,0,1:T(8,128)(2,1)}, u32[]{:S(2)}, u32[]{:S(2)}) async-start(bf16[48,8,256]{2,0,1:T(8,128)(2,1)} %bitcast.144), calls=%async_computation.1 | async-start | bytes 393216 | tf_op jit(solution)/shard_map/all_to_all | solution.py:180
  223.6 1.0 copy.55
  224.6 1.0 copy.57
  225.7 2.0 gather_fusion
  227.7 2.8 gather_fusion.1
  230.5 1.8 fusion.31
  232.3 15.1 %all-gather.11.cloned.1.call-done = bf16[3072,2,384]{2,1,0:T(2,128)(2,1)} async-done(((bf16[768,2,384]{2,1,0:T(2,128)(2,1)}), bf16[3072,2,384]{2,1,0:T(2,128)(2,1)}) %all-gather.11.cloned.1.call-update) | async-done | bytes 4718608 | tf_op jit(solution)/shard_map/all_gather | solution.py:182
  247.5 5.3 %copy.92 = bf16[384,8,2,384]{3,1,2,0:T(8,128)(2,1)} copy(bf16[384,8,2,384]{3,2,1,0:T(2,128)(2,1)} %bitcast.147) | data formatting | bytes 9437184
  252.8 1.0 reshape.283
  253.8 1.4 fusion.45
  255.2 1.9 multiply_reduce_fusion
  257.1 1.1 fusion.11
  259.2 1.0 broadcast_multiply_fusion
  260.2 1.1 copy.72
  261.2 2.8 gather_fusion.3
  264.0 2.1 copy.69
  266.0 2.7 gather_fusion.2
  268.8 1.4 multiply_reduce_fusion.2
  270.7 5.8 %convolution_convert_fusion = bf16[384,3072]{1,0:T(8,128)(2,1)} fusion(bf16[384,768]{0,1:T(8,128)(2,1)S(1)} %bitcast.153, bf16[3072,768]{1,0:T(8,128)(2,1)} %bitcast.148), kind=kOutput, calls=%fused_computation.4 | convolution fusion | flops 1813118976 | bytes 7667712 | tf_op jit(solution)/shard_map/dot_general | solution.py:81
  276.5 1.4 fusion.10
  278.2 18.6 %all_to_all.32 = bf16[8,48,256]{2,1,0:T(8,128)(2,1)S(1)} all-to-all(bf16[8,48,256]{2,1,0:T(8,128)(2,1)S(1)} %convert_element_type.131), channel_id=1, replica_groups=mesh['cand'=4,'seq'=8] {'seq'}, dimensions={0} | all-to-all | bytes 393216 | tf_op jit(solution)/shard_map/all_to_all | solution.py:175
  296.9 8.0 %fusion.2 = bf16[1,48,3072]{2,1,0:T(8,128)(2,1)} fusion(bf16[48,2048]{1,0:T(8,128)(2,1)S(1)} %bitcast.150, bf16[2048,3072]{1,0:T(8,128)(2,1)} %bitcast.146, bf16[1,48,3072]{2,1,0:T(8,128)(2,1)S(1)} %copy-done.2, f32[3072]{0:T(1024)S(1)} %bitcast.158), kind=kOutput, calls=%fused_computation.8 | convolution fusion | flops 604569600 | bytes 13381632 | tf_op jit(solution)/shard_map/dot_general | solution.py:176
  304.9 44.1 %reduce-scatter.2.cloned.1.call-done = bf16[48,3072]{1,0:T(8,128)(2,1)} async-done(((bf16[384,3072]{1,0:T(8,128)(2,1)}), bf16[48,3072]{1,0:T(8,128)(2,1)}) %reduce-scatter.2.cloned.1.call-update) | async-done | bytes 294928 | tf_op jit(solution)/shard_map/reduce_scatter | solution.py:183
  349.0 1.2 fusion.27
  350.2 2.0 fusion.24
  (88 shorter events, 4.7 us)
Async XLA Ops:
  7.2 3.0 copy-start
  7.2 44.2 %copy-start.2 = (bf16[1,48,3072]{2,1,0:T(8,128)(2,1)S(1)}, bf16[1,48,3072]{2,1,0:T(8,128)(2,1)}, u32[]{:S(2)}) copy-start(bf16[1,48,3072]{2,1,0:T(8,128)(2,1)} %param.13) | copy-start | bytes 884740
  7.2 66.0 %all-gather.7.cloned.1.call-start = ((), (), s32[]{:S(2)}) async-start(), calls=%async_computation.4 | async-start | bytes 3538944 | tf_op jit(solution)/shard_map/all_gather | solution.py:172
  7.9 126.1 %all-gather.5.cloned.1.call-start = ((), (), s32[]{:S(2)}) async-start(), calls=%async_computation.3 | async-start | bytes 2654208 | tf_op jit(solution)/shard_map/all_gather | solution.py:159
  51.4 21.9 %copy-start.5 = (bf16[768,2,384]{2,1,0:T(2,128)(2,1)S(1)}, bf16[768,2,384]{2,1,0:T(2,128)(2,1)}, u32[]{:S(2)}) copy-start(bf16[768,2,384]{2,1,0:T(2,128)(2,1)} %param.17) | copy-start | bytes 3538948
  52.7 155.9 %all-gather.9.cloned.1.call-start = ((), (), s32[]{:S(2)}) async-start(), calls=%async_computation.5 | async-start | bytes 15728640 | tf_op jit(solution)/shard_map/all_gather | solution.py:173
  73.2 33.5 %copy-start.18 = (s32[3,384]{1,0:T(4,128)S(1)}, s32[3,384]{1,0:T(4,128)}, u32[]{:S(2)}) copy-start(s32[3,384]{1,0:T(4,128)} %param.15) | copy-start | bytes 13828
  73.2 34.0 %copy-start.19 = (s32[128]{0:T(128)S(1)}, s32[128]{0:T(128)}, u32[]{:S(2)}) copy-start(s32[128]{0:T(128)} %constant.88) | copy-start | bytes 1540
  73.2 174.3 %all-gather.11.cloned.1.call-start = ((), (), s32[]{:S(2)}) async-start(), calls=%async_computation.6 | async-start | bytes 5898240 | tf_op jit(solution)/shard_map/all_gather | solution.py:182
  75.2 15.7 %collective-permute-start = (bf16[768,2,384]{0,2,1:T(8,128)(2,1)S(1)}, bf16[768,2,384]{0,2,1:T(8,128)(2,1)S(1)}, u32[]{:S(2)}, u32[]{:S(2)}) collective-permute-start(bf16[768,2,384]{0,2,1:T(8,128)(2,1)S(1)} %copy.51), channel_id=1, source_target_pairs={{0,8},{8,16},{16,24},{24,0},{1,9},{9,17},{17,25},{25,1},{2,10},{10... | collective-permute-start | bytes 3538952 | tf_op jit(solution)/shard_map/ppermute | solution.py:164
  90.9 15.7 %collective-permute-start.1 = (bf16[768,2,384]{0,2,1:T(8,128)(2,1)S(1)}, bf16[768,2,384]{0,2,1:T(8,128)(2,1)}, u32[]{:S(2)}, u32[]{:S(2)}) collective-permute-start(bf16[768,2,384]{0,2,1:T(8,128)(2,1)S(1)} %collective-permute-done), channel_id=1, source_target_pairs={{0,8},{8,16},{16,24},{24,0},{1,9},{9,17},{17,25},{25,1},{2,10},{10... | collective-permute-start | bytes 3538952 | tf_op jit(solution)/shard_map/ppermute | solution.py:164
  106.7 15.9 %collective-permute-start.2 = (bf16[768,2,384]{0,2,1:T(8,128)(2,1)}, bf16[768,2,384]{0,2,1:T(8,128)(2,1)}, u32[]{:S(2)}, u32[]{:S(2)}) collective-permute-start(bf16[768,2,384]{0,2,1:T(8,128)(2,1)} %collective-permute-done.1), channel_id=1, source_target_pairs={{0,8},{8,16},{16,24},{24,0},{1,9},{9,17},{17,25},{25,1},{2,10},{10... | collective-permute-start | bytes 3538952 | tf_op jit(solution)/shard_map/ppermute | solution.py:164
  107.9 17.5 %copy-start.8 = (f32[384,128]{0,1:T(8,128)}, f32[384,128]{0,1:T(8,128)S(1)}, u32[]{:S(2)}) copy-start(f32[384,128]{0,1:T(8,128)S(1)} %get-tuple-element.20) | copy-start | bytes 589828
  134.0 74.6 %copy-start.10 = (bf16[1,48,3072]{2,1,0:T(8,128)(2,1)S(1)}, bf16[1,48,3072]{2,1,0:T(8,128)(2,1)}, u32[]{:S(2)}) copy-start(bf16[1,48,3072]{2,1,0:T(8,128)(2,1)} %param.19) | copy-start | bytes 884740
  140.1 113.7 %copy-start.3 = (f32[3,2,384,128]{2,3,0,1:T(8,128)}, f32[3,2,384,128]{2,3,0,1:T(8,128)S(1)}, u32[]{:S(2)}) copy-start(f32[3,2,384,128]{2,3,0,1:T(8,128)S(1)} %fusion.5) | copy-start | bytes 3538948
  217.8 35.1 %all-to-all-start.1 = ((bf16[48,8,256]{2,0,1:T(8,128)(2,1)}), bf16[48,8,256]{2,0,1:T(8,128)(2,1)}, u32[]{:S(2)}, u32[]{:S(2)}) async-start(bf16[48,8,256]{2,0,1:T(8,128)(2,1)} %bitcast.144), calls=%async_computation.1 | async-start | bytes 393216 | tf_op jit(solution)/shard_map/all_to_all | solution.py:180
  223.3 125.7 %reduce-scatter.2.cloned.1.call-start = ((), (), s32[]{:S(2)}) async-start(), calls=%async_computation.7 | async-start | bytes 2654208 | tf_op jit(solution)/shard_map/reduce_scatter | solution.py:183
  223.5 7.0 %copy-start.9 = (f32[384,128]{0,1:T(8,128)S(1)}, f32[384,128]{0,1:T(8,128)}, u32[]{:S(2)}) copy-start(f32[384,128]{0,1:T(8,128)} %copy-done.8) | copy-start | bytes 589828
  223.5 7.0 %copy-start.17 = (f32[128]{0:T(128)S(1)}, f32[128]{0:T(128)}, u32[]{:S(2)}) copy-start(f32[128]{0:T(128)} %constant.82.clone) | copy-start | bytes 1540
  232.3 22.9 %copy-start.13 = (bf16[2,384,128]{1,2,0:T(8,128)(2,1)}, bf16[2,384,128]{1,2,0:T(8,128)(2,1)S(1)}, u32[]{:S(2)}) copy-start(bf16[2,384,128]{1,2,0:T(8,128)(2,1)S(1)} %get-tuple-element.14) | copy-start | bytes 589828
  247.5 7.8 %copy-start.15 = (bf16[2,384,128]{1,2,0:T(8,128)(2,1)S(1)}, bf16[2,384,128]{1,2,0:T(8,128)(2,1)}, u32[]{:S(2)}) copy-start(bf16[2,384,128]{1,2,0:T(8,128)(2,1)} %get-tuple-element.13) | copy-start | bytes 589828
  257.1 1.3 copy-start.4
  258.2 1.0 copy-start.14
  258.2 1.0 copy-start.16
  268.8 1.4 copy-start.6
  268.8 1.4 copy-start.7
  268.8 1.7 copy-start.12
  296.9 53.4 %copy-start.11 = (bf16[1,48,3072]{2,1,0:T(8,128)(2,1)S(1)}, bf16[1,48,3072]{2,1,0:T(8,128)(2,1)}, u32[]{:S(2)}) copy-start(bf16[1,48,3072]{2,1,0:T(8,128)(2,1)} %param.19) | copy-start | bytes 884740
  296.9 55.4 %copy-start.1 = (bf16[768,1152]{1,0:T(8,128)(2,1)S(1)}, bf16[768,1152]{1,0:T(8,128)(2,1)}, u32[]{:S(2)}) copy-start(bf16[768,1152]{1,0:T(8,128)(2,1)} %param.16) | copy-start | bytes 5308420
Sparse Core Ops, SparseCore 0:
  10.2 62.9 all-gather.6
  75.9 50.4 all-gather.4
  128.0 80.5 all-gather.8
  210.0 37.4 all-gather.10
  276.6 72.3 reduce-scatter.1
